TPU v7x, 512 devices: a whole 4x8x8 slice. The times are simulated.
512 devices in a mesh: dp: 64 (over y, x, core), tensor: 8 (over z).
Axes of the slice: x: 4, y: 8, z: 8, core: 2. Of those that a mesh axis runs over, the one named last changes fastest.
Arguments:
- hidden_act: bfloat16 [32768, 1408], P('dp', 'tensor'), may hold values from -6 to 6
- cotangent: bfloat16 [32768, 2048], P('dp', 'tensor'), may hold values from -4 to 4
- down_table: bfloat16 [1408, 64, 2048], P('tensor', 'dp'), may hold values from -0.15625 to 0.15625
- expert_ids: int32 [128, 4], P('dp'), may hold values from 0 to 31, as said below
- merge_weights: float32 [128, 4], P('dp'), may hold values from 0.1 to 1
- owner_slot: int32 [32], replicated, may hold values from 0 to 63, as said below
Outputs:
- layer_out: bfloat16 [32768, 2048], P('dp', 'tensor')
- grad_hidden: bfloat16 [32768, 1408], P('dp', 'tensor')
- expert_grad: float32 [1408, 64, 2048], P('tensor', 'dp')
Inputs may be any that keep to these rules, and one draw needn't show every extreme that they name: `expert_ids`: each segment lists 4 different experts; the 2 segments of one index of dp list exactly 6 different experts together. `owner_slot`: different experts have different slots; slot 63 always holds an expert.
All inputs are finite; a program needn't handle non-finite values.
Results may differ from a plain program's by a relative error of at most 0.013.
Values may be sent and summed in bfloat16 or wider, within the bound.
A program may use at most 128 MiB of HBM per device.

v0:
```python
import jax
import jax.numpy as jnp
from jax import lax
from jax.sharding import PartitionSpec as P

E = 32
K = 4
ROW_PARTS = 4
PAD = 4


def two_pieces(values):
    high = lax.reduce_precision(values, 8, 7)
    low = lax.reduce_precision(values - high, 8, 7)
    return (high, low)


def exchange(blocks):
    return lax.all_to_all(blocks, "dp", split_axis=0, concat_axis=0, tiled=True)


def split_panels(panels, count):
    lead, ff_local, width = panels.shape
    cols = count // ROW_PARTS
    view = panels.reshape(lead, ROW_PARTS, ff_local // ROW_PARTS, cols, width // cols)
    return jnp.transpose(view, (1, 3, 0, 2, 4)).reshape(
        count, lead, ff_local // ROW_PARTS, width // cols
    )


def join_panels(chunks):
    count, lead, rows, lanes = chunks.shape
    cols = count // ROW_PARTS
    view = chunks.reshape(ROW_PARTS, cols, lead, rows, lanes)
    return jnp.transpose(view, (2, 0, 3, 1, 4)).reshape(lead, ROW_PARTS * rows, cols * lanes)


def body(hidden_act, cotangent, down_table, expert_ids, merge_weights, owner_slot):
    count = lax.axis_size("dp")
    seg_count = expert_ids.shape[0]
    ff_local, _, width = down_table.shape
    row_count = hidden_act.shape[0]
    seg_len = row_count // seg_count
    rows = ff_local // ROW_PARTS
    lanes = width * ROW_PARTS // count
    listed = seg_count * K
    full_cot = lax.all_gather(cotangent, "tensor", axis=1, tiled=True)
    high, low = two_pieces(merge_weights)
    meta = jnp.concatenate(
        [expert_ids.astype(jnp.float32).reshape(-1), high.reshape(-1), low.reshape(-1)]
    ).astype(jnp.bfloat16)
    meta = jnp.pad(meta[None, :], ((0, PAD - 1), (0, lanes - 3 * listed)))
    table_chunks = split_panels(jnp.transpose(down_table, (1, 0, 2)), count)[:, 0]
    outgoing = jnp.concatenate(
        [table_chunks, jnp.broadcast_to(meta[None], (count, PAD, lanes))], axis=1
    )
    arrived = exchange(outgoing)
    by_slot = arrived[:, :rows]
    meta_all = arrived[:, rows, : 3 * listed].astype(jnp.float32)
    ids_all = meta_all[:, :listed].astype(jnp.int32).reshape(count * seg_count, K)
    high_all = meta_all[:, listed : 2 * listed].reshape(count * seg_count, K)
    low_all = meta_all[:, 2 * listed :].reshape(count * seg_count, K)
    experts = jnp.arange(E, dtype=jnp.int32)
    slots_all = jnp.sum(
        jnp.where(ids_all[:, :, None] == experts, owner_slot[None, None, :], 0), axis=2
    )
    hits = slots_all[:, :, None] == jnp.arange(count, dtype=jnp.int32)
    coef = jnp.concatenate(
        [
            jnp.sum(jnp.where(hits, high_all[:, :, None], 0.0), axis=1),
            jnp.sum(jnp.where(hits, low_all[:, :, None], 0.0), axis=1),
        ],
        axis=0,
    ).astype(jnp.bfloat16)
    halves = jnp.einsum("ms,srl->mrl", coef, by_slot, preferred_element_type=jnp.float32)
    merged_chunks = (halves[: count * seg_count] + halves[count * seg_count :]).astype(jnp.bfloat16)
    merged = join_panels(exchange(merged_chunks.reshape(count, seg_count, rows, lanes)))
    hidden_seg = hidden_act.reshape(seg_count, seg_len, ff_local)
    cot_seg = full_cot.reshape(seg_count, seg_len, width)
    seg_grads = jnp.einsum(
        "stf,std->sfd", hidden_seg, cot_seg, preferred_element_type=jnp.float32
    ).astype(jnp.bfloat16)
    returned = exchange(split_panels(seg_grads, count)).reshape(count * seg_count, rows, lanes)
    partial_rows = jnp.einsum(
        "stf,sfd->std", hidden_seg, merged, preferred_element_type=jnp.float32
    ).reshape(row_count, width)
    layer_out = lax.psum_scatter(
        partial_rows.astype(jnp.bfloat16), "tensor", scatter_dimension=1, tiled=True
    )
    grad_hidden = (
        jnp.einsum("std,sfd->stf", cot_seg, merged, preferred_element_type=jnp.float32)
        .astype(jnp.bfloat16)
        .reshape(row_count, ff_local)
    )
    by_segment = jnp.stack([coef[: count * seg_count], coef[count * seg_count :]], axis=1)
    slot_halves = jnp.einsum(
        "mhs,mrl->hsrl", by_segment, returned, preferred_element_type=jnp.float32
    )
    slot_grads = (slot_halves[0] + slot_halves[1]).astype(jnp.bfloat16)
    own_grad = join_panels(exchange(slot_grads)[:, None])
    expert_grad = jnp.transpose(own_grad, (1, 0, 2)).astype(jnp.float32)
    return (layer_out, grad_hidden, expert_grad)


def solution(mesh):
    placed = (
        P("dp", "tensor"),
        P("dp", "tensor"),
        P("tensor", "dp", None),
        P("dp", None),
        P("dp", None),
        P(),
    )
    return jax.shard_map(
        body,
        mesh=mesh,
        in_specs=placed,
        out_specs=(P("dp", "tensor"), P("dp", "tensor"), P("tensor", "dp", None)),
        check_vma=False,
    )
```

profile of v0, /device:TPU:1, one launch (start us, length us, event | category | flops | bytes accessed | tf_op | source)
XLA Modules:
  0.0 178.1 jit_solution(396525168196531516)
XLA Ops:
  7.2 0.7 reduce-precision_convert_fusion
  8.0 0.7 convert_convert_fusion
  8.8 1.3 copy.65
  10.4 1.0 pad_maximum_fusion
  11.4 11.8 %all-to-all-start = ((bf16[64,48,128]{2,1,0:T(8,128)(2,1)}), bf16[64,48,128]{2,1,0:T(8,128)(2,1)S(1)}, u32[]{:S(2)}, u32[]{:S(2)}) async-start(bf16[64,48,128]{2,1,0:T(8,128)(2,1)} %pad_maximum_fusion), calls=%async_computation | async-start | bytes 1572864 | tf_op jit(solution)/shard_map/all_to_all | solution.py:19
  23.2 0.7 all-gather.2.cloned.1.call-update
  23.9 22.0 %all-to-all-done = bf16[64,48,128]{2,1,0:T(8,128)(2,1)S(1)} async-done(((bf16[64,48,128]{2,1,0:T(8,128)(2,1)}), bf16[64,48,128]{2,1,0:T(8,128)(2,1)S(1)}, u32[]{:S(2)}, u32[]{:S(2)}) %all-to-all-start) | async-done | bytes 786464 | tf_op jit(solution)/shard_map/all_to_all | solution.py:19
  46.6 0.9 fusion.4
  47.5 0.5 fusion
  48.1 2.1 %copy.51 = bf16[64,2,44,128]{3,1,2,0:T(2,128)(2,1)} copy(bf16[64,2,44,128]{3,1,0,2:T(2,128)(2,1)S(1)} %bitcast.66) | data formatting | bytes 2883584 | tf_op jit(solution)/shard_map/reshape | solution.py:77
  50.2 6.4 %all-to-all-start.1 = ((bf16[64,2,44,128]{3,1,2,0:T(2,128)(2,1)}), bf16[64,2,44,128]{3,1,2,0:T(2,128)(2,1)S(1)}, u32[]{:S(2)}, u32[]{:S(2)}) async-start(bf16[64,2,44,128]{3,1,2,0:T(2,128)(2,1)} %copy.51), calls=%async_computation.1 | async-start | bytes 2883584 | tf_op jit(solution)/shard_map/all_to_all | solution.py:19
  56.6 20.5 %all-gather.2.cloned.1.call-done = bf16[512,2048]{1,0:T(8,128)(2,1)} async-done(((bf16[512,256]{1,0:T(8,128)(2,1)}), bf16[512,2048]{1,0:T(8,128)(2,1)}) %all-gather.2.cloned.1.call-update) | async-done | bytes 2097168 | tf_op jit(solution)/shard_map/all_gather | solution.py:47
  77.1 2.1 %convolution_convert_fusion.1 = bf16[2,176,2048]{2,1,0:T(8,128)(2,1)S(1)} fusion(bf16[2,256,2048]{2,1,0:T(8,128)(2,1)} %bitcast.63, bf16[22,2,8,256]{3,2,1,0:T(8,128)(2,1)S(1)} %bitcast.77), kind=kOutput, calls=%fused_computation.3 | convolution fusion | flops 369819648 | bytes 3719168 | tf_op jit(solution)/shard_map/stf,std->sfd/dot_general | solution.py:80
  79.2 0.4 copy.66
  79.6 0.4 copy.56
  80.0 2.6 %copy.57 = bf16[64,2,44,128]{3,1,2,0:T(2,128)(2,1)} copy(bf16[64,2,44,128]{3,0,2,1:T(8,128)(2,1)S(1)} %bitcast.71) | data formatting | bytes 2883584 | tf_op jit(solution)/shard_map/reshape | solution.py:26
  82.6 10.3 %all-to-all-done.1 = bf16[64,2,44,128]{3,1,2,0:T(2,128)(2,1)S(1)} async-done(((bf16[64,2,44,128]{3,1,2,0:T(2,128)(2,1)}), bf16[64,2,44,128]{3,1,2,0:T(2,128)(2,1)S(1)}, u32[]{:S(2)}, u32[]{:S(2)}) %all-to-all-start.1) | async-done | bytes 1441824 | tf_op jit(solution)/shard_map/all_to_all | solution.py:19
  92.9 6.3 %all-to-all-start.2 = ((bf16[64,2,44,128]{3,1,2,0:T(2,128)(2,1)}), bf16[64,2,44,128]{3,1,2,0:T(2,128)(2,1)S(1)}, u32[]{:S(2)}, u32[]{:S(2)}) async-start(bf16[64,2,44,128]{3,1,2,0:T(2,128)(2,1)} %copy.57), calls=%async_computation.3 | async-start | bytes 2883584 | tf_op jit(solution)/shard_map/all_to_all | solution.py:19
  99.4 1.3 copy.78
  100.7 2.5 %reshape.114 = bf16[2,176,2048]{2,1,0:T(8,128)(2,1)S(1)} reshape(bf16[2,4,44,16,128]{4,3,2,1,0:T(8,128)(2,1)} %bitcast.72) | data formatting | bytes 2883584 | tf_op jit(solution)/shard_map/reshape | solution.py:35
  103.2 2.1 %convolution_convert_fusion = bf16[2,2048,256]{1,2,0:T(8,128)(2,1)} fusion(bf16[2,176,2048]{2,1,0:T(8,128)(2,1)S(1)} %reshape.114, bf16[22,2,8,256]{3,2,1,0:T(8,128)(2,1)S(1)} %bitcast.78), kind=kOutput, calls=%fused_computation | convolution fusion | flops 370147328 | bytes 3719168 | tf_op jit(solution)/shard_map/stf,sfd->std/dot_general | solution.py:84
  105.3 30.3 %all-to-all-done.2 = bf16[64,2,44,128]{3,1,2,0:T(2,128)(2,1)S(1)} async-done(((bf16[64,2,44,128]{3,1,2,0:T(2,128)(2,1)}), bf16[64,2,44,128]{3,1,2,0:T(2,128)(2,1)S(1)}, u32[]{:S(2)}, u32[]{:S(2)}) %all-to-all-start.2) | async-done | bytes 1441824 | tf_op jit(solution)/shard_map/all_to_all | solution.py:19
  135.6 1.5 copy.58
  137.1 0.5 fusion.12
  137.6 0.3 fusion.3
  137.9 1.4 copy.59
  139.3 6.5 %all-to-all-start.3 = ((bf16[64,44,128]{2,1,0:T(8,128)(2,1)}), bf16[64,44,128]{2,1,0:T(8,128)(2,1)}, u32[]{:S(2)}, u32[]{:S(2)}) async-start(bf16[64,44,128]{2,1,0:T(8,128)(2,1)} %copy.59), calls=%async_computation.4 | async-start | bytes 1572864 | tf_op jit(solution)/shard_map/all_to_all | solution.py:19
  145.8 0.8 fusion.2
  146.6 0.7 copy.64
  147.3 21.1 %all-to-all-done.3 = bf16[64,44,128]{2,1,0:T(8,128)(2,1)} async-done(((bf16[64,44,128]{2,1,0:T(8,128)(2,1)}), bf16[64,44,128]{2,1,0:T(8,128)(2,1)}, u32[]{:S(2)}, u32[]{:S(2)}) %all-to-all-start.3) | async-done | bytes 720928 | tf_op jit(solution)/shard_map/all_to_all | solution.py:19
  168.5 1.3 convert_bitcast_fusion
  169.7 1.5 copy.60
  (26 shorter events, 1.6 us)
Async XLA Ops:
  11.4 35.1 %copy-start.2 = (s32[32]{0:T(128)S(1)}, s32[32]{0:T(128)}, u32[]{:S(2)}) copy-start(s32[32]{0:T(128)} %param.11) | copy-start | bytes 388
  11.4 34.5 %all-to-all-start = ((bf16[64,48,128]{2,1,0:T(8,128)(2,1)}), bf16[64,48,128]{2,1,0:T(8,128)(2,1)S(1)}, u32[]{:S(2)}, u32[]{:S(2)}) async-start(bf16[64,48,128]{2,1,0:T(8,128)(2,1)} %pad_maximum_fusion), calls=%async_computation | async-start | bytes 1572864 | tf_op jit(solution)/shard_map/all_to_all | solution.py:19
  23.1 54.0 %all-gather.2.cloned.1.call-start = ((), (), s32[]{:S(2)}) async-start(), calls=%async_computation.6 | async-start | bytes 2359296 | tf_op jit(solution)/shard_map/all_gather | solution.py:47
  50.2 26.9 %copy-start.1 = (bf16[512,176]{0,1:T(8,128)(2,1)S(1)}, bf16[512,176]{0,1:T(8,128)(2,1)}, u32[]{:S(2)}) copy-start(bf16[512,176]{0,1:T(8,128)(2,1)} %param.6) | copy-start | bytes 540676
  50.2 42.7 %all-to-all-start.1 = ((bf16[64,2,44,128]{3,1,2,0:T(2,128)(2,1)}), bf16[64,2,44,128]{3,1,2,0:T(2,128)(2,1)S(1)}, u32[]{:S(2)}, u32[]{:S(2)}) async-start(bf16[64,2,44,128]{3,1,2,0:T(2,128)(2,1)} %copy.51), calls=%async_computation.1 | async-start | bytes 2883584 | tf_op jit(solution)/shard_map/all_to_all | solution.py:19
  92.9 42.7 %all-to-all-start.2 = ((bf16[64,2,44,128]{3,1,2,0:T(2,128)(2,1)}), bf16[64,2,44,128]{3,1,2,0:T(2,128)(2,1)S(1)}, u32[]{:S(2)}, u32[]{:S(2)}) async-start(bf16[64,2,44,128]{3,1,2,0:T(2,128)(2,1)} %copy.57), calls=%async_computation.3 | async-start | bytes 2883584 | tf_op jit(solution)/shard_map/all_to_all | solution.py:19
  99.2 72.1 %reduce-scatter.2.cloned.1.call-start = ((), (), s32[]{:S(2)}) async-start(), calls=%async_computation.5 | async-start | bytes 2359296 | tf_op jit(solution)/shard_map/reduce_scatter | solution.py:87
  137.9 7.8 %copy-start = (bf16[512,2048]{1,0:T(8,128)(2,1)S(1)}, bf16[512,2048]{1,0:T(8,128)(2,1)}, u32[]{:S(2)}) copy-start(bf16[512,2048]{1,0:T(8,128)(2,1)} %all-gather.2.cloned.1.call-done) | copy-start | bytes 6291460
  139.3 29.2 %all-to-all-start.3 = ((bf16[64,44,128]{2,1,0:T(8,128)(2,1)}), bf16[64,44,128]{2,1,0:T(8,128)(2,1)}, u32[]{:S(2)}, u32[]{:S(2)}) async-start(bf16[64,44,128]{2,1,0:T(8,128)(2,1)} %copy.59), calls=%async_computation.4 | async-start | bytes 1572864 | tf_op jit(solution)/shard_map/all_to_all | solution.py:19
Sparse Core Ops, SparseCore 0:
  26.0 51.0 all-gather.1
  105.4 45.6 reduce-scatter.1
where the time goes:
time: 179 us; the launch traced here: 178 us
  waiting for transfers between devices  105 us (59%)
  starting transfers between devices  31.1 us (17%)
  local copies, waits for them, and re-layouts  16.5 us (9%)
  between operations  14.2 us (8%)
  matrix products  6.5 us (4%)
  other arithmetic  4.78 us (3%)
    all_to_all x4, waiting for transfers between devices, exchange(): return lax.all_to_all(blocks, 'dp', split_axis=0, concat_axis=0, tiled=True)  83.7 us
    all_to_all x4, starting transfers between devices, exchange(): return lax.all_to_all(blocks, 'dp', split_axis=0, concat_axis=0, tiled=True)  30.9 us
    all_gather x1, waiting for transfers between devices, body(): full_cot = lax.all_gather(cotangent, 'tensor', axis=1, tiled=True)  20.5 us
  transfers between devices with their start and end apart: 6, of which 5 were waited for; matrix products, arithmetic and copies ran while one was open for 13% of the time, Pallas kernels for 0%

commit v1 on v0

--- a/solution.py
+++ b/solution.py
@@ -44,7 +44,13 @@
     rows = ff_local // ROW_PARTS
     lanes = width * ROW_PARTS // count
     listed = seg_count * K
-    full_cot = lax.all_gather(cotangent, "tensor", axis=1, tiled=True)
+    count_2 = lax.axis_size("tensor")
+    current, pieces = (cotangent, [cotangent])
+    for _ in range(count_2 - 1):
+        current = lax.ppermute(current, "tensor", [(i, (i + 1) % count_2) for i in range(count_2)])
+        pieces.insert(0, current)
+    line = jnp.concatenate(pieces, axis=1)
+    full_cot = jnp.roll(line, (lax.axis_index("tensor") + 1) * cotangent.shape[1], axis=1)
     high, low = two_pieces(merge_weights)
     meta = jnp.concatenate(
         [expert_ids.astype(jnp.float32).reshape(-1), high.reshape(-1), low.reshape(-1)]

time: 179 us -> 222 us (1.24)
  starting transfers between devices: 31.1 us -> 55.5 us
  waiting for transfers between devices: 105 us -> 121 us
  local copies, waits for them, and re-layouts: 16.5 us -> 19 us
    ppermute x0 -> x7, waiting for transfers between devices: none -> 50 us  [body(): lax.ppermute(current, 'tensor', [(i, (i + 1) % count_2) for i in range(co...]
    all_gather x1 -> x0, waiting for transfers between devices: 20.5 us -> none  [body(): full_cot = lax.all_gather(cotangent, 'tensor', axis=1, tiled=True)]
    ppermute x0 -> x7, starting transfers between devices: none -> 15.5 us  [body(): lax.ppermute(current, 'tensor', [(i, (i + 1) % count_2) for i in range(co...]
    all_to_all x4, waiting for transfers between devices: 83.7 us -> 70.5 us  [exchange(): return lax.all_to_all(blocks, 'dp', split_axis=0, concat_axis=0, tiled=True)]
    all_to_all x4, starting transfers between devices: 30.9 us -> 39.8 us  [exchange(): return lax.all_to_all(blocks, 'dp', split_axis=0, concat_axis=0, tiled=True)]
  transfers between devices with their start and end apart: 6 -> 12, of which waited for: 5 -> 9; matrix products, arithmetic and copies ran while one was open for 13% -> 12% of each run, Pallas kernels for 0% -> 0%
where the time goes in v1:
time: 222 us; the launch traced here: 221 us
  waiting for transfers between devices  121 us (55%)
  starting transfers between devices  55.5 us (25%)
  local copies, waits for them, and re-layouts  19 us (9%)
  between operations  14.5 us (7%)
  matrix products  6.57 us (3%)
  other arithmetic  4.82 us (2%)
    all_to_all x4, waiting for transfers between devices, exchange(): return lax.all_to_all(blocks, 'dp', split_axis=0, concat_axis=0, tiled=True)  70.5 us
    ppermute x7, waiting for transfers between devices, body(): lax.ppermute(current, 'tensor', [(i, (i + 1) % count_2) for i in range(co...  50 us
    all_to_all x4, starting transfers between devices, exchange(): return lax.all_to_all(blocks, 'dp', split_axis=0, concat_axis=0, tiled=True)  39.8 us
    ppermute x7, starting transfers between devices, body(): lax.ppermute(current, 'tensor', [(i, (i + 1) % count_2) for i in range(co...  15.5 us
  transfers between devices with their start and end apart: 12, of which 9 were waited for; matrix products, arithmetic and copies ran while one was open for 12% of the time, Pallas kernels for 0%

profile of v1, /device:TPU:1, one launch (start us, length us, event | category | flops | bytes accessed | tf_op | source)
XLA Modules:
  0.0 220.9 jit_solution(5024835127686759877)
XLA Ops:
  8.8 1.3 copy.65
  10.4 1.0 pad_maximum_fusion
  11.4 11.6 %all-to-all-start = ((bf16[64,48,128]{2,1,0:T(8,128)(2,1)}), bf16[64,48,128]{2,1,0:T(8,128)(2,1)S(1)}, u32[]{:S(2)}, u32[]{:S(2)}) async-start(bf16[64,48,128]{2,1,0:T(8,128)(2,1)} %pad_maximum_fusion), calls=%async_computation | async-start | bytes 1572864 | tf_op jit(solution)/shard_map/all_to_all | solution.py:19
  23.1 4.0 %collective-permute-start = (bf16[512,256]{1,0:T(8,128)(2,1)S(1)}, bf16[512,256]{1,0:T(8,128)(2,1)S(1)}, u32[]{:S(2)}, u32[]{:S(2)}) collective-permute-start(bf16[512,256]{1,0:T(8,128)(2,1)S(1)} %copy-done), channel_id=1, source_target_pairs={{0,1},{1,2},{2,3},{3,4},{4,5},{5,6},{6,7},{7,0},{8,9},{9,10},{10,1... | collective-permute-start | bytes 786440 | tf_op jit(solution)/shard_map/ppermute | solution.py:50
  27.1 12.9 %collective-permute-done = bf16[512,256]{1,0:T(8,128)(2,1)S(1)} collective-permute-done((bf16[512,256]{1,0:T(8,128)(2,1)S(1)}, bf16[512,256]{1,0:T(8,128)(2,1)S(1)}, u32[]{:S(2)}, u32[]{:S(2)}) %collective-permute-start) | collective-permute-done | bytes 262176 | tf_op jit(solution)/shard_map/ppermute | solution.py:50
  40.0 1.9 collective-permute-start.1
  41.9 8.0 %collective-permute-done.1 = bf16[512,256]{1,0:T(8,128)(2,1)S(1)} collective-permute-done((bf16[512,256]{1,0:T(8,128)(2,1)S(1)}, bf16[512,256]{1,0:T(8,128)(2,1)S(1)}, u32[]{:S(2)}, u32[]{:S(2)}) %collective-permute-start.1) | collective-permute-done | bytes 262176 | tf_op jit(solution)/shard_map/ppermute | solution.py:50
  49.9 1.9 collective-permute-start.2
  51.8 7.1 %collective-permute-done.2 = bf16[512,256]{1,0:T(8,128)(2,1)S(1)} collective-permute-done((bf16[512,256]{1,0:T(8,128)(2,1)S(1)}, bf16[512,256]{1,0:T(8,128)(2,1)S(1)}, u32[]{:S(2)}, u32[]{:S(2)}) %collective-permute-start.2) | collective-permute-done | bytes 262176 | tf_op jit(solution)/shard_map/ppermute | solution.py:50
  58.9 1.9 collective-permute-start.3
  60.8 6.4 %collective-permute-done.3 = bf16[512,256]{1,0:T(8,128)(2,1)S(1)} collective-permute-done((bf16[512,256]{1,0:T(8,128)(2,1)S(1)}, bf16[512,256]{1,0:T(8,128)(2,1)S(1)}, u32[]{:S(2)}, u32[]{:S(2)}) %collective-permute-start.3) | collective-permute-done | bytes 262176 | tf_op jit(solution)/shard_map/ppermute | solution.py:50
  67.2 1.9 collective-permute-start.4
  69.2 6.4 %collective-permute-done.4 = bf16[512,256]{1,0:T(8,128)(2,1)S(1)} collective-permute-done((bf16[512,256]{1,0:T(8,128)(2,1)S(1)}, bf16[512,256]{1,0:T(8,128)(2,1)S(1)}, u32[]{:S(2)}, u32[]{:S(2)}) %collective-permute-start.4) | collective-permute-done | bytes 262176 | tf_op jit(solution)/shard_map/ppermute | solution.py:50
  75.6 1.9 collective-permute-start.5
  79.7 2.1 copy.51
  81.8 15.3 %all-to-all-start.1 = ((bf16[64,2,44,128]{3,1,2,0:T(2,128)(2,1)}), bf16[64,2,44,128]{3,1,2,0:T(2,128)(2,1)S(1)}, u32[]{:S(2)}, u32[]{:S(2)}) async-start(bf16[64,2,44,128]{3,1,2,0:T(2,128)(2,1)} %copy.51), calls=%async_computation.1 | async-start | bytes 2883584 | tf_op jit(solution)/shard_map/all_to_all | solution.py:19
  97.1 1.9 collective-permute-start.6
  99.1 9.2 %collective-permute-done.6 = bf16[512,256]{1,0:T(8,128)(2,1)S(1)} collective-permute-done((bf16[512,256]{1,0:T(8,128)(2,1)S(1)}, bf16[512,256]{1,0:T(8,128)(2,1)S(1)}, u32[]{:S(2)}, u32[]{:S(2)}) %collective-permute-start.6) | collective-permute-done | bytes 262176 | tf_op jit(solution)/shard_map/ppermute | solution.py:50
  110.8 2.6 %copy.57 = bf16[64,2,44,128]{3,1,2,0:T(2,128)(2,1)} copy(bf16[64,2,44,128]{3,0,2,1:T(8,128)(2,1)S(1)} %bitcast.71) | data formatting | bytes 2883584 | tf_op jit(solution)/shard_map/reshape | solution.py:26
  113.4 20.1 %all-to-all-done.1 = bf16[64,2,44,128]{3,1,2,0:T(2,128)(2,1)S(1)} async-done(((bf16[64,2,44,128]{3,1,2,0:T(2,128)(2,1)}), bf16[64,2,44,128]{3,1,2,0:T(2,128)(2,1)S(1)}, u32[]{:S(2)}, u32[]{:S(2)}) %all-to-all-start.1) | async-done | bytes 1441824 | tf_op jit(solution)/shard_map/all_to_all | solution.py:19
  133.5 6.5 %all-to-all-start.2 = ((bf16[64,2,44,128]{3,1,2,0:T(2,128)(2,1)}), bf16[64,2,44,128]{3,1,2,0:T(2,128)(2,1)}, u32[]{:S(2)}, u32[]{:S(2)}) async-start(bf16[64,2,44,128]{3,1,2,0:T(2,128)(2,1)} %copy.57), calls=%async_computation.3 | async-start | bytes 2883584 | tf_op jit(solution)/shard_map/all_to_all | solution.py:19
  140.2 1.3 copy.78
  141.4 2.5 %reshape.114 = bf16[2,176,2048]{2,1,0:T(8,128)(2,1)S(1)} reshape(bf16[2,4,44,16,128]{4,3,2,1,0:T(8,128)(2,1)} %bitcast.72) | data formatting | bytes 2883584 | tf_op jit(solution)/shard_map/reshape | solution.py:35
  143.9 3.0 %convolution_convert_fusion = bf16[2,2048,256]{1,2,0:T(8,128)(2,1)} fusion(bf16[2,176,2048]{2,1,0:T(8,128)(2,1)S(1)} %reshape.114, bf16[22,2,8,256]{3,2,1,0:T(8,128)(2,1)} %bitcast.77), kind=kOutput, calls=%fused_computation | convolution fusion | flops 370147328 | bytes 3719168 | tf_op jit(solution)/shard_map/stf,sfd->std/dot_general | solution.py:90
  146.9 29.3 %all-to-all-done.2 = bf16[64,2,44,128]{3,1,2,0:T(2,128)(2,1)} async-done(((bf16[64,2,44,128]{3,1,2,0:T(2,128)(2,1)}), bf16[64,2,44,128]{3,1,2,0:T(2,128)(2,1)}, u32[]{:S(2)}, u32[]{:S(2)}) %all-to-all-start.2) | async-done | bytes 1441824 | tf_op jit(solution)/shard_map/all_to_all | solution.py:19
  176.2 2.9 %copy.58 = bf16[64,2,44,128]{3,1,0,2:T(2,128)(2,1)S(1)} copy(bf16[64,2,44,128]{3,1,2,0:T(2,128)(2,1)} %all-to-all-done.2) | data formatting | bytes 2883584 | tf_op jit(solution)/shard_map/all_to_all | solution.py:19
  179.1 1.2 fusion.12
  180.7 1.4 copy.59
  182.0 6.5 %all-to-all-start.3 = ((bf16[64,44,128]{2,1,0:T(8,128)(2,1)}), bf16[64,44,128]{2,1,0:T(8,128)(2,1)}, u32[]{:S(2)}, u32[]{:S(2)}) async-start(bf16[64,44,128]{2,1,0:T(8,128)(2,1)} %copy.59), calls=%async_computation.4 | async-start | bytes 1572864 | tf_op jit(solution)/shard_map/all_to_all | solution.py:19
  190.0 21.2 %all-to-all-done.3 = bf16[64,44,128]{2,1,0:T(8,128)(2,1)} async-done(((bf16[64,44,128]{2,1,0:T(8,128)(2,1)}), bf16[64,44,128]{2,1,0:T(8,128)(2,1)}, u32[]{:S(2)}, u32[]{:S(2)}) %all-to-all-start.3) | async-done | bytes 720928 | tf_op jit(solution)/shard_map/all_to_all | solution.py:19
  211.2 1.3 convert_bitcast_fusion
  212.5 1.5 copy.60
  (56 shorter events, 8.6 us)
Async XLA Ops:
  7.2 15.9 %copy-start = (bf16[512,256]{1,0:T(8,128)(2,1)S(1)}, bf16[512,256]{1,0:T(8,128)(2,1)}, u32[]{:S(2)}) copy-start(bf16[512,256]{1,0:T(8,128)(2,1)} %param.7) | copy-start | bytes 786436
  7.2 70.9 %copy-start.3 = (s32[32]{0:T(128)S(1)}, s32[32]{0:T(128)}, u32[]{:S(2)}) copy-start(s32[32]{0:T(128)} %param.11) | copy-start | bytes 388
  11.4 66.1 %all-to-all-start = ((bf16[64,48,128]{2,1,0:T(8,128)(2,1)}), bf16[64,48,128]{2,1,0:T(8,128)(2,1)S(1)}, u32[]{:S(2)}, u32[]{:S(2)}) async-start(bf16[64,48,128]{2,1,0:T(8,128)(2,1)} %pad_maximum_fusion), calls=%async_computation | async-start | bytes 1572864 | tf_op jit(solution)/shard_map/all_to_all | solution.py:19
  23.1 16.9 %collective-permute-start = (bf16[512,256]{1,0:T(8,128)(2,1)S(1)}, bf16[512,256]{1,0:T(8,128)(2,1)S(1)}, u32[]{:S(2)}, u32[]{:S(2)}) collective-permute-start(bf16[512,256]{1,0:T(8,128)(2,1)S(1)} %copy-done), channel_id=1, source_target_pairs={{0,1},{1,2},{2,3},{3,4},{4,5},{5,6},{6,7},{7,0},{8,9},{9,10},{10,1... | collective-permute-start | bytes 786440 | tf_op jit(solution)/shard_map/ppermute | solution.py:50
  40.0 9.9 %collective-permute-start.1 = (bf16[512,256]{1,0:T(8,128)(2,1)S(1)}, bf16[512,256]{1,0:T(8,128)(2,1)S(1)}, u32[]{:S(2)}, u32[]{:S(2)}) collective-permute-start(bf16[512,256]{1,0:T(8,128)(2,1)S(1)} %collective-permute-done), channel_id=1, source_target_pairs={{0,1},{1,2},{2,3},{3,4},{4,5},{5,6},{6,7},{7,0},{8,9},{9,10},{10,1... | collective-permute-start | bytes 786440 | tf_op jit(solution)/shard_map/ppermute | solution.py:50
  49.9 9.0 %collective-permute-start.2 = (bf16[512,256]{1,0:T(8,128)(2,1)S(1)}, bf16[512,256]{1,0:T(8,128)(2,1)S(1)}, u32[]{:S(2)}, u32[]{:S(2)}) collective-permute-start(bf16[512,256]{1,0:T(8,128)(2,1)S(1)} %collective-permute-done.1), channel_id=1, source_target_pairs={{0,1},{1,2},{2,3},{3,4},{4,5},{5,6},{6,7},{7,0},{8,9},{9,10},{10,1... | collective-permute-start | bytes 786440 | tf_op jit(solution)/shard_map/ppermute | solution.py:50
  58.9 8.3 %collective-permute-start.3 = (bf16[512,256]{1,0:T(8,128)(2,1)S(1)}, bf16[512,256]{1,0:T(8,128)(2,1)S(1)}, u32[]{:S(2)}, u32[]{:S(2)}) collective-permute-start(bf16[512,256]{1,0:T(8,128)(2,1)S(1)} %collective-permute-done.2), channel_id=1, source_target_pairs={{0,1},{1,2},{2,3},{3,4},{4,5},{5,6},{6,7},{7,0},{8,9},{9,10},{10,1... | collective-permute-start | bytes 786440 | tf_op jit(solution)/shard_map/ppermute | solution.py:50
  67.2 8.3 %collective-permute-start.4 = (bf16[512,256]{1,0:T(8,128)(2,1)S(1)}, bf16[512,256]{1,0:T(8,128)(2,1)S(1)}, u32[]{:S(2)}, u32[]{:S(2)}) collective-permute-start(bf16[512,256]{1,0:T(8,128)(2,1)S(1)} %collective-permute-done.3), channel_id=1, source_target_pairs={{0,1},{1,2},{2,3},{3,4},{4,5},{5,6},{6,7},{7,0},{8,9},{9,10},{10,1... | collective-permute-start | bytes 786440 | tf_op jit(solution)/shard_map/ppermute | solution.py:50
  75.6 21.5 %collective-permute-start.5 = (bf16[512,256]{1,0:T(8,128)(2,1)S(1)}, bf16[512,256]{1,0:T(8,128)(2,1)S(1)}, u32[]{:S(2)}, u32[]{:S(2)}) collective-permute-start(bf16[512,256]{1,0:T(8,128)(2,1)S(1)} %collective-permute-done.4), channel_id=1, source_target_pairs={{0,1},{1,2},{2,3},{3,4},{4,5},{5,6},{6,7},{7,0},{8,9},{9,10},{10,1... | collective-permute-start | bytes 786440 | tf_op jit(solution)/shard_map/ppermute | solution.py:50
  78.2 1.5 copy-start.2
  81.8 51.6 %all-to-all-start.1 = ((bf16[64,2,44,128]{3,1,2,0:T(2,128)(2,1)}), bf16[64,2,44,128]{3,1,2,0:T(2,128)(2,1)S(1)}, u32[]{:S(2)}, u32[]{:S(2)}) async-start(bf16[64,2,44,128]{3,1,2,0:T(2,128)(2,1)} %copy.51), calls=%async_computation.1 | async-start | bytes 2883584 | tf_op jit(solution)/shard_map/all_to_all | solution.py:19
  97.1 11.1 %collective-permute-start.6 = (bf16[512,256]{1,0:T(8,128)(2,1)S(1)}, bf16[512,256]{1,0:T(8,128)(2,1)S(1)}, u32[]{:S(2)}, u32[]{:S(2)}) collective-permute-start(bf16[512,256]{1,0:T(8,128)(2,1)S(1)} %collective-permute-done.5), channel_id=1, source_target_pairs={{0,1},{1,2},{2,3},{3,4},{4,5},{5,6},{6,7},{7,0},{8,9},{9,10},{10,1... | collective-permute-start | bytes 786440 | tf_op jit(solution)/shard_map/ppermute | solution.py:50
  108.5 0.9 copy-start.1
  133.5 42.8 %all-to-all-start.2 = ((bf16[64,2,44,128]{3,1,2,0:T(2,128)(2,1)}), bf16[64,2,44,128]{3,1,2,0:T(2,128)(2,1)}, u32[]{:S(2)}, u32[]{:S(2)}) async-start(bf16[64,2,44,128]{3,1,2,0:T(2,128)(2,1)} %copy.57), calls=%async_computation.3 | async-start | bytes 2883584 | tf_op jit(solution)/shard_map/all_to_all | solution.py:19
  139.9 74.1 %reduce-scatter.2.cloned.1.call-start = ((), (), s32[]{:S(2)}) async-start(), calls=%async_computation.5 | async-start | bytes 2359296 | tf_op jit(solution)/shard_map/reduce_scatter | solution.py:93
  182.0 29.2 %all-to-all-start.3 = ((bf16[64,44,128]{2,1,0:T(8,128)(2,1)}), bf16[64,44,128]{2,1,0:T(8,128)(2,1)}, u32[]{:S(2)}, u32[]{:S(2)}) async-start(bf16[64,44,128]{2,1,0:T(8,128)(2,1)} %copy.59), calls=%async_computation.4 | async-start | bytes 1572864 | tf_op jit(solution)/shard_map/all_to_all | solution.py:19
Sparse Core Ops, SparseCore 0:
  147.1 39.7 reduce-scatter.1
